TPU v7x, 32 devices: a whole 2x2x4 slice. The times are simulated.
32 devices in a mesh: row: 2 (over core), pitch: 4 (over y, x), span: 4 (over z).
Axes of the slice: x: 2, y: 2, z: 4, core: 2. Of those that a mesh axis runs over, the one named last changes fastest.
Arguments:
- snapshots: bfloat16 [2, 20, 3, 32, 256, 256], P('row', None, None, 'pitch', 'span'), may hold values from -6 to 6
- snap_index: int32 [16], replicated, may hold values from 0 to 19, as said below
- flow_state: float32 [2, 5, 32, 256, 256], P('row', None, 'pitch', 'span'), may hold values from -6 to 6
- eddy_viscosity: float32 [2, 32, 256, 256], P('row', 'pitch', 'span'), may hold values from 0.04 to 0.4
- intersection: int32 [2, 32], P('row'), may hold values from 0 to 31, as said below
- counts: int32 [2, 32], P('row'), may hold values from 1 to 8, as said below
Outputs:
- received_stress: float32 [2, 6, 256, 256], P('row', None, 'span')
- new_state: float32 [2, 5, 32, 256, 256], P('row', None, 'pitch', 'span')
Inputs may be any that keep to these rules, and one draw needn't show every extreme that they name: `snap_index`: 16 distinct slots, among them slot 0 and slot 19. `intersection`: for each row, a one-to-one map of blocks. Call blocks k * 8 to (k + 1) * 8 - 1 group k: the blocks of one group take their sources from at most 2 blocks of any one group of the other layout, and exactly 2 for some pairs of groups. `counts`: each row has a block with all 8 cells live.
All inputs are finite; a program needn't handle non-finite values.
Results may differ from a plain program's by a relative error of at most 0.0003.
Values sent between devices are 32-bit elements; how exact they have to be, the bound alone decides.
A program may use at most 128 MiB of HBM per device.

v0:
```python
import jax
import jax.numpy as jnp
from jax import lax
from jax.sharding import PartitionSpec as P

SNAPS = 16
BLOCK = 8
CAPACITY = 2
stress_pairs = ((0, 0), (0, 1), (0, 2), (1, 1), (1, 2), (2, 2))
time_step = 0.1


def padded_2(block, sides, width, periodic):
    for axis, dim in sides:
        count = lax.axis_size(axis)
        forward = [(i, i + 1) for i in range(count - 1)]
        if periodic:
            forward.append((count - 1, 0))
        backward = [(target, source) for source, target in forward]
        low = lax.ppermute(
            lax.slice_in_dim(block, block.shape[dim] - width, None, axis=dim), axis, forward
        )
        high = lax.ppermute(lax.slice_in_dim(block, 0, width, axis=dim), axis, backward)
        block = jnp.concatenate([low, block, high], axis=dim)
    return block


def partner(block, axis, bit):
    count = lax.axis_size(axis)
    route = []
    for low in range(count):
        high = low | 1 << bit
        if high != low and high < count:
            route += [(low, high), (high, low)]
    return lax.ppermute(block, axis, route)


def axial_diff(values):
    padded = jnp.concatenate([values[..., :1], values, values[..., -1:]], axis=-1)
    return (padded[..., 2:] - padded[..., :-2]) * 0.5


def residual(flow_field, speed, viscosity, live_mask, forcing):
    around_pitch = padded_2(flow_field, (("pitch", 1),), 1, True)
    around_span = padded_2(flow_field, (("span", 2),), 1, False)
    axial_pad = jnp.concatenate([flow_field[..., :1], flow_field, flow_field[..., -1:]], axis=3)
    laplace = (
        around_pitch[:, 2:]
        + around_pitch[:, :-2]
        + around_span[:, :, 2:]
        + around_span[:, :, :-2]
        + axial_pad[..., 2:]
        + axial_pad[..., :-2]
        - 6.0 * flow_field
    )
    return live_mask * (-axial_diff(speed * flow_field) + viscosity * laplace + forcing)


def deliver(values, block_links):
    swapped = partner(values, "row", 0)
    span_count = lax.axis_size("span")
    blocks_all = block_links.shape[0]
    per_dev = blocks_all // span_count
    share_len = swapped.shape[2]
    block_len = swapped.shape[1] // per_dev
    position = lax.axis_index("span")
    block_ids = jnp.arange(blocks_all, dtype=jnp.int32)
    pairing = (block_links[:, None] == block_ids[None, :]).astype(jnp.int32)
    target = jnp.sum(pairing * block_ids[:, None], axis=0)
    target_dev = target // per_dev
    source_dev = block_ids // per_dev
    earlier = (
        (source_dev[:, None] == source_dev[None, :])
        & (target_dev[:, None] == target_dev[None, :])
        & (block_ids[None, :] < block_ids[:, None])
    )
    slot_of = jnp.sum(earlier.astype(jnp.int32), axis=1)
    devices = jnp.arange(span_count, dtype=jnp.int32)
    places = jnp.arange(CAPACITY, dtype=jnp.int32)
    my_dev = lax.dynamic_slice_in_dim(target_dev, position * per_dev, per_dev)
    my_slot = lax.dynamic_slice_in_dim(slot_of, position * per_dev, per_dev)
    placing = (
        (my_dev[:, None, None] == devices[None, :, None])
        & (my_slot[:, None, None] == places[None, None, :])
    ).astype(jnp.float32)
    blocks = swapped.reshape(6, per_dev, block_len * share_len)
    outgoing = jnp.einsum("jnc,mjw->ncmw", placing, blocks, precision=lax.Precision.HIGHEST)
    incoming = lax.all_to_all(outgoing, "span", split_axis=0, concat_axis=0, tiled=True)
    wanted = lax.dynamic_slice_in_dim(block_links, position * per_dev, per_dev)
    from_dev = wanted // per_dev
    from_slot = jnp.sum(
        (wanted[:, None] == block_ids[None, :]).astype(jnp.int32) * slot_of[None, :], axis=1
    )
    choosing = (
        (from_dev[:, None, None] == devices[None, :, None])
        & (from_slot[:, None, None] == places[None, None, :])
    ).astype(jnp.float32)
    arrived = jnp.einsum("knc,ncmw->mkw", choosing, incoming, precision=lax.Precision.HIGHEST)
    return arrived.reshape(6, per_dev * block_len, share_len)


def body(snapshots, snap_index, flow_state, eddy_viscosity, intersection, counts):
    stored = snapshots[0]
    start = flow_state[0]
    viscosity = eddy_viscosity[0]
    block_links = intersection[0]
    block_counts = counts[0]
    pitch_cells = stored.shape[2]
    span_cells = stored.shape[3]
    axial_cells = stored.shape[4]
    pitch_total = pitch_cells * lax.axis_size("pitch")

    def select_slot(slot):
        return lax.dynamic_index_in_dim(stored, slot, 0, keepdims=False).astype(jnp.float32)

    def add_mean(step_num, running):
        return running + select_slot(snap_index[step_num])

    running = lax.fori_loop(0, SNAPS, add_mean, jnp.zeros(stored.shape[1:], jnp.float32))
    time_mean = running / SNAPS

    def add_products(step_num, running):
        fluct = select_slot(snap_index[step_num]) - time_mean
        return running + jnp.stack([jnp.sum(fluct[p] * fluct[q], axis=0) for p, q in stress_pairs])

    summed = lax.fori_loop(
        0, SNAPS, add_products, jnp.zeros((6, span_cells, axial_cells), jnp.float32)
    )
    partial_value = summed / (SNAPS * pitch_total)
    totals = lax.psum(partial_value, "pitch")
    received = deliver(totals, block_links)
    position = lax.axis_index("span")
    span_total = span_cells * lax.axis_size("span")
    span_pos = (
        (position * span_cells + jnp.arange(span_cells, dtype=jnp.int32)).astype(jnp.float32) + 0.5
    ) / span_total
    curvature = (1.0 / (1.0 + span_pos))[:, None]
    source_x = -axial_diff(received[0]) - curvature * received[1]
    source_r = -axial_diff(received[1]) + curvature * (received[5] - received[3])
    source_t = -axial_diff(received[2]) - 2.0 * curvature * received[4]
    energy = time_mean[0] * source_x + time_mean[1] * source_r + time_mean[2] * source_t
    forcing = jnp.concatenate(
        [
            jnp.zeros((1, pitch_cells, span_cells, axial_cells), jnp.float32),
            jnp.broadcast_to(
                jnp.stack([source_x, source_r, source_t])[:, None],
                (3, pitch_cells, span_cells, axial_cells),
            ),
            energy[None],
        ],
        axis=0,
    )
    per_dev = span_cells // BLOCK
    my_counts = lax.dynamic_slice_in_dim(block_counts, position * per_dev, per_dev)
    live_mask = (jnp.arange(BLOCK, dtype=jnp.int32)[None, :] < my_counts[:, None]).astype(
        jnp.float32
    )
    live_mask = live_mask.reshape(span_cells)[:, None]
    speed = 0.5 + time_mean[0]
    section_one = start + time_step * residual(start, speed, viscosity, live_mask, forcing)
    finished = 0.5 * (
        start
        + section_one
        + time_step * residual(section_one, speed, viscosity, live_mask, forcing)
    )
    return (received[None], finished[None])


def solution(mesh):
    return jax.shard_map(
        body,
        mesh=mesh,
        in_specs=(
            P("row", None, None, "pitch", "span", None),
            P(),
            P("row", None, "pitch", "span", None),
            P("row", "pitch", "span", None),
            P("row", None),
            P("row", None),
        ),
        out_specs=(P("row", None, "span", None), P("row", None, "pitch", "span", None)),
        check_vma=False,
    )
```

profile of v0, /device:TPU:0, one launch (start us, length us, event | category | flops | bytes accessed | tf_op | source)
XLA Modules:
  0.0 288.5 jit_solution(12164644477243232642)
XLA Ops:
  7.2 1.8 fusion.64
  10.3 6.2 %collective-permute-start.4 = (f32[5,8,1,256]{3,2,1,0:T(1,128)}, f32[5,8,1,256]{3,2,1,0:T(1,128)}, u32[]{:S(2)}, u32[]{:S(2)}) collective-permute-start(f32[5,8,1,256]{3,2,1,0:T(1,128)} %get-tuple-element.251), channel_id=1, source_target_pairs={{0,1},{1,2},{2,3},{4,5},{5,6},{6,7},{8,9},{9,10},{10,11},{12,13},{... | collective-permute-start | bytes 122888 | tf_op jit(solution)/shard_map/ppermute | solution.py:20
  16.5 2.0 fusion.63
  18.4 2.9 collective-permute-start.1
  21.3 77.6 %while.28 = (s32[]{:T(128)}, f32[3,8,64,256]{3,2,1,0:T(8,128)S(1)}, s32[16]{0:T(128)}, bf16[20,3,8,64,256]{4,3,2,1,0:T(8,128)(2,1)}, s32[]{:T(128)}, /*index=5*/s32[]{:T(128)}, s32[]{:T(128)}) while((s32[]{:T(128)}, f32[3,8,64,256]{3,2,1,0:T(8,128)S(1)}, s32[16]{0:T(128)}, bf16[20,3,8,64,256]{4,3,2,1,0:T(8,128)(2,1)}, s32[]{:T(128)}, ...), condition=%wide.region_3.0_spmd.clone, body=%wide.region_2.3_spmd.clone.sunk | while | flops 1179654 | bytes 3932305 | solution.py:119
  24.5 1.7 convert_add_fusion.2
  29.3 1.7 convert_add_fusion.2
  34.2 1.7 convert_add_fusion.2
  39.0 1.7 convert_add_fusion.2
  43.9 1.7 convert_add_fusion.2
  48.7 1.7 convert_add_fusion.2
  53.6 1.7 convert_add_fusion.2
  58.4 1.7 convert_add_fusion.2
  63.3 1.7 convert_add_fusion.2
  68.1 1.7 convert_add_fusion.2
  73.0 1.7 convert_add_fusion.2
  77.8 1.7 convert_add_fusion.2
  82.7 1.7 convert_add_fusion.2
  87.5 1.7 convert_add_fusion.2
  92.4 1.7 convert_add_fusion.2
  97.2 1.7 convert_add_fusion.2
  99.6 69.6 %while.29 = (s32[]{:T(128)}, f32[6,64,256]{2,1,0:T(8,128)S(1)}, s32[16]{0:T(128)S(1)}, bf16[20,3,8,64,256]{4,3,2,1,0:T(8,128)(2,1)}, f32[3,8,64,256]{3,2,1,0:T(8,128)S(1)}, /*index=5*/s32[]{:T(128)}, s32[]{:T(128)}, s32[]{:T(128)}) while((s32[]{:T(128)}, f32[6,64,256]{2,1,0:T(8,128)S(1)}, s32[16]{0:T(128)S(1)}, ...), condition=%wide.region_11.12_spmd.clone, body=%wide.region_4.11_spmd.clone.sunk | while | flops 2457606 | bytes 7864473 | solution.py:126
  102.1 1.4 convert_subtract_fusion.2
  106.4 1.4 convert_subtract_fusion.2
  110.8 1.4 convert_subtract_fusion.2
  115.1 1.4 convert_subtract_fusion.2
  119.5 1.4 convert_subtract_fusion.2
  123.8 1.4 convert_subtract_fusion.2
  128.2 1.4 convert_subtract_fusion.2
  132.5 1.4 convert_subtract_fusion.2
  136.9 1.4 convert_subtract_fusion.2
  141.2 1.4 convert_subtract_fusion.2
  145.6 1.4 convert_subtract_fusion.2
  149.9 1.4 convert_subtract_fusion.2
  170.7 44.2 %all-reduce.2.cloned.1.call-done = f32[6,64,256]{2,1,0:T(8,128)} async-done(((f32[6,64,256]{2,1,0:T(8,128)}), f32[6,64,256]{2,1,0:T(8,128)}) %all-reduce.2.cloned.1.call-update) | async-done | bytes 393232 | tf_op jit(solution)/shard_map/psum | solution.py:130
  215.0 1.9 collective-permute-done
  218.2 4.6 %all-to-all-start = ((f32[4,2,6,2048]{3,1,2,0:T(2,128)}), f32[4,2,6,2048]{3,1,2,0:T(2,128)S(1)}, u32[]{:S(2)}, u32[]{:S(2)}) async-start(f32[4,2,6,2048]{3,1,2,0:T(2,128)} %fusion.48), calls=%async_computation | async-start | bytes 786432 | tf_op jit(solution)/shard_map/all_to_all | solution.py:88
  222.9 3.2 %fusion.65 = (f32[5,8,64,1]{3,2,1,0:T(8,128)S(1)}, f32[5,8,64,1]{3,2,1,0:T(8,128)}) fusion(f32[5,8,64,256]{3,2,1,0:T(8,128)} %bitcast.77), kind=kLoop, calls=%fused_computation.139 | loop fusion | bytes 40960 | tf_op jit(solution)/shard_map/slice | solution.py:46
  226.1 8.6 %all-to-all-done = f32[4,2,6,2048]{3,1,2,0:T(2,128)S(1)} async-done(((f32[4,2,6,2048]{3,1,2,0:T(2,128)}), f32[4,2,6,2048]{3,1,2,0:T(2,128)S(1)}, u32[]{:S(2)}, u32[]{:S(2)}) %all-to-all-start) | async-done | bytes 393248 | tf_op jit(solution)/shard_map/all_to_all | solution.py:88
  238.3 2.0 fusion.62
  240.5 6.7 %broadcast_multiply_fusion = (f32[5,8,64,256]{3,2,1,0:T(8,128)S(1)}, f32[5,8,64,256]{3,2,1,0:T(8,128)S(1)}) fusion(f32[8,64,256]{2,1,0:T(8,128)S(1)} %get-tuple-element.255, f32[5,8,64,256]{3,2,1,0:T(8,128)S(1)} %bitcast.78, f32[1,8,64,256]{3,2,1,0:T(8,128)S(1)} %get-tuple-element.254, f32[3,8,64,256]{3,2,1,0:T(8,128)S(1)} %broadcast_in_dim.13, ...), kind=kLoop, calls=%fused_computation.65 | loop fusion | flops 17694720 | bytes 14410004 | tf_op jit(solution)/shard_map/mul | solution.py:56
  248.3 1.9 fusion.61
  250.2 1.5 collective-permute-start.5
  254.2 4.5 %collective-permute-start.8 = (f32[5,8,1,256]{3,2,1,0:T(1,128)S(1)}, f32[5,8,1,256]{3,2,1,0:T(1,128)S(1)}, u32[]{:S(2)}, u32[]{:S(2)}) collective-permute-start(f32[5,8,1,256]{3,2,1,0:T(1,128)S(1)} %get-tuple-element.243), channel_id=1, source_target_pairs={{0,1},{1,2},{2,3},{4,5},{5,6},{6,7},{8,9},{9,10},{10,11},{12,13},{... | collective-permute-start | bytes 122888 | tf_op jit(solution)/shard_map/ppermute | solution.py:20
  258.7 1.9 fusion.58
  260.7 1.8 broadcast_in_dim_reshape.3
  262.5 4.6 %collective-permute-done.6 = f32[5,1,64,256]{3,2,1,0:T(8,128)} collective-permute-done((f32[5,1,64,256]{3,2,1,0:T(8,128)}, f32[5,1,64,256]{3,2,1,0:T(8,128)}, u32[]{:S(2)}, u32[]{:S(2)}) %collective-permute-start.6) | collective-permute-done | bytes 327712 | tf_op jit(solution)/shard_map/ppermute | solution.py:20
  267.0 14.6 %fusion.9 = f32[1,5,8,64,256]{4,3,2,1,0:T(8,128)} fusion(f32[5,8,64,256]{3,2,1,0:T(8,128)} %copy-done.2, f32[5,8,64,1]{3,2,1,0:T(8,128)} %get-tuple-element.245, f32[5,8,64,1]{3,2,1,0:T(8,128)S(1)} %get-tuple-element.244, f32[5,8,1,256]{3,2,1,0:T(1,128)S(1)} %collective-permute-done.8, f32[5,8,1,256]{3,2,1,0:T(1,128)S(1)} %collective-permute-done.7, ...), kind=kLoop, calls=%fused_computation.25 | loop fusion | flops 18350080 | bytes 13885716 | tf_op jit(solution)/shard_map/broadcast_in_dim | solution.py:166
  (232 shorter events, 53.5 us)
Async XLA Ops:
  7.2 162.8 %copy-start = (s32[1,32]{1,0:T(1,128)S(1)}, s32[1,32]{1,0:T(1,128)}, u32[]{:S(2)}) copy-start(s32[1,32]{1,0:T(1,128)} %param.15) | copy-start | bytes 388
  7.2 207.7 %all-reduce.2.cloned.1.call-start = ((), (), s32[]{:S(2)}) async-start(), calls=%async_computation.1 | async-start | bytes 786432 | tf_op jit(solution)/shard_map/psum | solution.py:130
  9.0 231.3 %collective-permute-start.3 = (f32[5,8,1,256]{3,2,1,0:T(1,128)}, f32[5,8,1,256]{3,2,1,0:T(1,128)}, u32[]{:S(2)}, u32[]{:S(2)}) collective-permute-start(f32[5,8,1,256]{3,2,1,0:T(1,128)} %get-tuple-element.250), channel_id=1, source_target_pairs={{1,0},{2,1},{3,2},{5,4},{6,5},{7,6},{9,8},{10,9},{11,10},{13,12},{... | collective-permute-start | bytes 122888 | tf_op jit(solution)/shard_map/ppermute | solution.py:23
  10.3 230.1 %collective-permute-start.4 = (f32[5,8,1,256]{3,2,1,0:T(1,128)}, f32[5,8,1,256]{3,2,1,0:T(1,128)}, u32[]{:S(2)}, u32[]{:S(2)}) collective-permute-start(f32[5,8,1,256]{3,2,1,0:T(1,128)} %get-tuple-element.251), channel_id=1, source_target_pairs={{0,1},{1,2},{2,3},{4,5},{5,6},{6,7},{8,9},{9,10},{10,11},{12,13},{... | collective-permute-start | bytes 122888 | tf_op jit(solution)/shard_map/ppermute | solution.py:20
  18.4 221.9 %collective-permute-start.1 = (f32[5,1,64,256]{3,2,1,0:T(8,128)}, f32[5,1,64,256]{3,2,1,0:T(8,128)}, u32[]{:S(2)}, u32[]{:S(2)}) collective-permute-start(f32[5,1,64,256]{3,2,1,0:T(8,128)} %get-tuple-element.248), channel_id=1, source_target_pairs={{4,0},{8,4},{12,8},{0,12},{5,1},{9,5},{13,9},{1,13},{6,2},{10,6},{... | collective-permute-start | bytes 983048 | tf_op jit(solution)/shard_map/ppermute | solution.py:23
  21.3 219.0 %collective-permute-start.2 = (f32[5,1,64,256]{3,2,1,0:T(8,128)}, f32[5,1,64,256]{3,2,1,0:T(8,128)}, u32[]{:S(2)}, u32[]{:S(2)}) collective-permute-start(f32[5,1,64,256]{3,2,1,0:T(8,128)} %get-tuple-element.249), channel_id=1, source_target_pairs={{0,4},{4,8},{8,12},{12,0},{1,5},{5,9},{9,13},{13,1},{2,6},{6,10},{... | collective-permute-start | bytes 983048 | tf_op jit(solution)/shard_map/ppermute | solution.py:20
  98.9 0.7 copy-start.6
  99.5 70.5 %copy-start.5 = (s32[1,32]{1,0:T(1,128)S(1)}, s32[1,32]{1,0:T(1,128)}, u32[]{:S(2)}) copy-start(s32[1,32]{1,0:T(1,128)} %param.14) | copy-start | bytes 388
  214.9 1.9 collective-permute-start
  218.2 16.6 %all-to-all-start = ((f32[4,2,6,2048]{3,1,2,0:T(2,128)}), f32[4,2,6,2048]{3,1,2,0:T(2,128)S(1)}, u32[]{:S(2)}, u32[]{:S(2)}) async-start(f32[4,2,6,2048]{3,1,2,0:T(2,128)} %fusion.48), calls=%async_computation | async-start | bytes 786432 | tf_op jit(solution)/shard_map/all_to_all | solution.py:88
  235.3 0.8 copy-start.4
  236.3 1.7 copy-start.1
  247.3 4.9 %copy-start.2 = (f32[5,8,64,256]{3,2,1,0:T(8,128)}, f32[5,8,64,256]{3,2,1,0:T(8,128)S(1)}, u32[]{:S(2)}) copy-start(f32[5,8,64,256]{3,2,1,0:T(8,128)S(1)} %get-tuple-element.235) | copy-start | bytes 7864324
  247.3 11.5 %copy-start.3 = (f32[5,8,64,256]{3,2,1,0:T(8,128)}, f32[5,8,64,256]{3,2,1,0:T(8,128)S(1)}, u32[]{:S(2)}) copy-start(f32[5,8,64,256]{3,2,1,0:T(8,128)S(1)} %get-tuple-element.234) | copy-start | bytes 7864324
  250.2 12.3 %collective-permute-start.5 = (f32[5,1,64,256]{3,2,1,0:T(8,128)}, f32[5,1,64,256]{3,2,1,0:T(8,128)}, u32[]{:S(2)}, u32[]{:S(2)}) collective-permute-start(f32[5,1,64,256]{3,2,1,0:T(8,128)} %get-tuple-element.240), channel_id=1, source_target_pairs={{4,0},{8,4},{12,8},{0,12},{5,1},{9,5},{13,9},{1,13},{6,2},{10,6},{... | collective-permute-start | bytes 983048 | tf_op jit(solution)/shard_map/ppermute | solution.py:23
  251.6 15.4 %collective-permute-start.6 = (f32[5,1,64,256]{3,2,1,0:T(8,128)}, f32[5,1,64,256]{3,2,1,0:T(8,128)}, u32[]{:S(2)}, u32[]{:S(2)}) collective-permute-start(f32[5,1,64,256]{3,2,1,0:T(8,128)} %get-tuple-element.241), channel_id=1, source_target_pairs={{0,4},{4,8},{8,12},{12,0},{1,5},{5,9},{9,13},{13,1},{2,6},{6,10},{... | collective-permute-start | bytes 983048 | tf_op jit(solution)/shard_map/ppermute | solution.py:20
  252.9 9.6 %collective-permute-start.7 = (f32[5,8,1,256]{3,2,1,0:T(1,128)}, f32[5,8,1,256]{3,2,1,0:T(1,128)S(1)}, u32[]{:S(2)}, u32[]{:S(2)}) collective-permute-start(f32[5,8,1,256]{3,2,1,0:T(1,128)} %get-tuple-element.242), channel_id=1, source_target_pairs={{1,0},{2,1},{3,2},{5,4},{6,5},{7,6},{9,8},{10,9},{11,10},{13,12},{... | collective-permute-start | bytes 122888 | tf_op jit(solution)/shard_map/ppermute | solution.py:23
  254.2 8.3 %collective-permute-start.8 = (f32[5,8,1,256]{3,2,1,0:T(1,128)S(1)}, f32[5,8,1,256]{3,2,1,0:T(1,128)S(1)}, u32[]{:S(2)}, u32[]{:S(2)}) collective-permute-start(f32[5,8,1,256]{3,2,1,0:T(1,128)S(1)} %get-tuple-element.243), channel_id=1, source_target_pairs={{0,1},{1,2},{2,3},{4,5},{5,6},{6,7},{8,9},{9,10},{10,11},{12,13},{... | collective-permute-start | bytes 122888 | tf_op jit(solution)/shard_map/ppermute | solution.py:20
Sparse Core Ops, SparseCore 0:
  170.0 44.8 all-reduce.1
where the time goes:
time: 291 us; the launch traced here: 289 us
  other arithmetic  77.3 us (27%)
  loops' own time  63.3 us (22%)
  waiting for transfers between devices  59.3 us (20%)
  local copies, waits for them, and re-layouts  49.7 us (17%)
  starting transfers between devices  22.9 us (8%)
  between operations  14.3 us (5%)
    psum x1, waiting for transfers between devices, body(): totals = lax.psum(partial_value, 'pitch')  44.2 us
    another operation x1, loops' own time, body(): lax.fori_loop(0, SNAPS, add_products, jnp.zeros((6, span_cells, axial_cel...  32.4 us
    another operation x1, loops' own time, body(): lax.fori_loop(0, SNAPS, add_mean, jnp.zeros(stored.shape[1:], jnp.float32))  30.9 us
    add x16, other arithmetic, add_mean(): return running + select_slot(snap_index[step_num])  26.5 us
    sub x16, other arithmetic, add_products(): fluct = select_slot(snap_index[step_num]) - time_mean  21.6 us
    dynamic_slice x16, local copies, waits for them, and re-layouts, add_mean(): return running + select_slot(snap_index[step_num])  20.2 us
    broadcast_in_dim x1, other arithmetic, body(): return (received[None], finished[None])  14.6 us
    ppermute x4, starting transfers between devices, padded_2(): lax.ppermute(lax.slice_in_dim(block, block.shape[dim] - width, None, axis...  11.3 us
  transfers between devices with their start and end apart: 11, of which 4 were waited for; matrix products, arithmetic and copies ran while one was open for 35% of the time, Pallas kernels for 0%

commit v1 on v0

--- a/solution.py
+++ b/solution.py
@@ -127,7 +127,7 @@
         0, SNAPS, add_products, jnp.zeros((6, span_cells, axial_cells), jnp.float32)
     )
     partial_value = summed / (SNAPS * pitch_total)
-    totals = lax.psum(partial_value, "pitch")
+    totals = jnp.sum(lax.all_gather(partial_value, "pitch"), axis=0)
     received = deliver(totals, block_links)
     position = lax.axis_index("span")
     span_total = span_cells * lax.axis_size("span")

time: 291 us -> 276 us (0.948)
  waiting for transfers between devices: 59.3 us -> 42.1 us
    psum x1 -> x0, waiting for transfers between devices: 44.2 us -> none  [body(): totals = lax.psum(partial_value, 'pitch')]
    all_gather x0 -> x1, waiting for transfers between devices: none -> 26.6 us  [body(): totals = jnp.sum(lax.all_gather(partial_value, 'pitch'), axis=0)]
  transfers between devices with their start and end apart: 11 -> 11, of which waited for: 4 -> 4; matrix products, arithmetic and copies ran while one was open for 35% -> 7% of each run, Pallas kernels for 0% -> 0%
where the time goes in v1:
time: 276 us; the launch traced here: 273 us
  other arithmetic  79.5 us (29%)
  loops' own time  63.3 us (23%)
  local copies, waits for them, and re-layouts  49.7 us (18%)
  waiting for transfers between devices  42.1 us (15%)
  starting transfers between devices  21.9 us (8%)
  between operations  14.4 us (5%)
    another operation x1, loops' own time, body(): lax.fori_loop(0, SNAPS, add_products, jnp.zeros((6, span_cells, axial_cel...  32.4 us
    another operation x1, loops' own time, body(): lax.fori_loop(0, SNAPS, add_mean, jnp.zeros(stored.shape[1:], jnp.float32))  30.9 us
    all_gather x1, waiting for transfers between devices, body(): totals = jnp.sum(lax.all_gather(partial_value, 'pitch'), axis=0)  26.6 us
    add x16, other arithmetic, add_mean(): return running + select_slot(snap_index[step_num])  26.5 us
    sub x16, other arithmetic, add_products(): fluct = select_slot(snap_index[step_num]) - time_mean  21.6 us
    dynamic_slice x16, local copies, waits for them, and re-layouts, add_mean(): return running + select_slot(snap_index[step_num])  20.2 us
    broadcast_in_dim x1, other arithmetic, body(): return (received[None], finished[None])  14.8 us
    ppermute x4, starting transfers between devices, padded_2(): lax.ppermute(lax.slice_in_dim(block, block.shape[dim] - width, None, axis...  10.7 us
  transfers between devices with their start and end apart: 11, of which 4 were waited for; matrix products, arithmetic and copies ran while one was open for 7% of the time, Pallas kernels for 0%

profile of v1, /device:TPU:0, one launch (start us, length us, event | category | flops | bytes accessed | tf_op | source)
XLA Modules:
  0.0 272.7 jit_solution(1790245470005030771)
XLA Ops:
  7.2 77.6 %while.28 = (s32[]{:T(128)}, f32[3,8,64,256]{3,2,1,0:T(8,128)S(1)}, s32[16]{0:T(128)}, bf16[20,3,8,64,256]{4,3,2,1,0:T(8,128)(2,1)}, s32[]{:T(128)}, /*index=5*/s32[]{:T(128)}, s32[]{:T(128)}) while((s32[]{:T(128)}, f32[3,8,64,256]{3,2,1,0:T(8,128)S(1)}, s32[16]{0:T(128)}, bf16[20,3,8,64,256]{4,3,2,1,0:T(8,128)(2,1)}, s32[]{:T(128)}, ...), condition=%wide.region_3.0_spmd.clone, body=%wide.region_2.3_spmd.clone.sunk | while | flops 1179654 | bytes 3932305 | solution.py:119
  10.4 1.7 convert_add_fusion.2
  15.3 1.7 convert_add_fusion.2
  20.1 1.7 convert_add_fusion.2
  25.0 1.7 convert_add_fusion.2
  29.8 1.7 convert_add_fusion.2
  34.7 1.7 convert_add_fusion.2
  39.5 1.7 convert_add_fusion.2
  44.4 1.7 convert_add_fusion.2
  49.2 1.7 convert_add_fusion.2
  54.1 1.7 convert_add_fusion.2
  58.9 1.7 convert_add_fusion.2
  63.8 1.7 convert_add_fusion.2
  68.6 1.7 convert_add_fusion.2
  73.5 1.7 convert_add_fusion.2
  78.3 1.7 convert_add_fusion.2
  83.2 1.7 convert_add_fusion.2
  85.5 69.6 %while.29 = (s32[]{:T(128)}, f32[6,64,256]{2,1,0:T(8,128)S(1)}, s32[16]{0:T(128)S(1)}, bf16[20,3,8,64,256]{4,3,2,1,0:T(8,128)(2,1)}, f32[3,8,64,256]{3,2,1,0:T(8,128)S(1)}, /*index=5*/s32[]{:T(128)}, s32[]{:T(128)}, s32[]{:T(128)}) while((s32[]{:T(128)}, f32[6,64,256]{2,1,0:T(8,128)S(1)}, s32[16]{0:T(128)S(1)}, ...), condition=%wide.region_11.12_spmd.clone, body=%wide.region_4.11_spmd.clone.sunk | while | flops 2457606 | bytes 7864473 | solution.py:126
  88.0 1.4 convert_subtract_fusion.2
  92.4 1.4 convert_subtract_fusion.2
  96.7 1.4 convert_subtract_fusion.2
  101.1 1.4 convert_subtract_fusion.2
  105.4 1.4 convert_subtract_fusion.2
  109.8 1.4 convert_subtract_fusion.2
  114.1 1.4 convert_subtract_fusion.2
  118.5 1.4 convert_subtract_fusion.2
  122.8 1.4 convert_subtract_fusion.2
  127.2 1.4 convert_subtract_fusion.2
  131.5 1.4 convert_subtract_fusion.2
  155.9 1.7 fusion.64
  158.9 5.6 %collective-permute-start.4 = (f32[5,8,1,256]{3,2,1,0:T(1,128)S(1)}, f32[5,8,1,256]{3,2,1,0:T(1,128)S(1)}, u32[]{:S(2)}, u32[]{:S(2)}) collective-permute-start(f32[5,8,1,256]{3,2,1,0:T(1,128)S(1)} %get-tuple-element.251), channel_id=1, source_target_pairs={{0,1},{1,2},{2,3},{4,5},{5,6},{6,7},{8,9},{9,10},{10,11},{12,13},{... | collective-permute-start | bytes 122888 | tf_op jit(solution)/shard_map/ppermute | solution.py:20
  164.5 2.0 fusion.63
  166.5 2.9 %collective-permute-start.1 = (f32[5,1,64,256]{3,2,1,0:T(8,128)}, f32[5,1,64,256]{3,2,1,0:T(8,128)}, u32[]{:S(2)}, u32[]{:S(2)}) collective-permute-start(f32[5,1,64,256]{3,2,1,0:T(8,128)} %get-tuple-element.248), channel_id=1, source_target_pairs={{4,0},{8,4},{12,8},{0,12},{5,1},{9,5},{13,9},{1,13},{6,2},{10,6},{... | collective-permute-start | bytes 983048 | tf_op jit(solution)/shard_map/ppermute | solution.py:23
  170.2 26.6 %all-gather.3.cloned.1.call-done = f32[24,64,256]{2,1,0:T(8,128)} async-done(((f32[6,64,256]{2,1,0:T(8,128)}), f32[24,64,256]{2,1,0:T(8,128)}) %all-gather.3.cloned.1.call-update) | async-done | bytes 1572880 | tf_op jit(solution)/shard_map/all_gather | solution.py:130
  196.8 1.6 reduce_sum.116
  198.5 1.6 collective-permute-done
  201.5 4.1 %all-to-all-start = ((f32[4,2,6,2048]{3,1,2,0:T(2,128)}), f32[4,2,6,2048]{3,1,2,0:T(2,128)S(1)}, u32[]{:S(2)}, u32[]{:S(2)}) async-start(f32[4,2,6,2048]{3,1,2,0:T(2,128)} %fusion.48), calls=%async_computation | async-start | bytes 786432 | tf_op jit(solution)/shard_map/all_to_all | solution.py:88
  205.8 3.2 %fusion.65 = (f32[5,8,64,1]{3,2,1,0:T(8,128)S(1)}, f32[5,8,64,1]{3,2,1,0:T(8,128)}) fusion(f32[5,8,64,256]{3,2,1,0:T(8,128)} %bitcast.78), kind=kLoop, calls=%fused_computation.139 | loop fusion | bytes 40960 | tf_op jit(solution)/shard_map/slice | solution.py:46
  209.0 8.6 %all-to-all-done = f32[4,2,6,2048]{3,1,2,0:T(2,128)S(1)} async-done(((f32[4,2,6,2048]{3,1,2,0:T(2,128)}), f32[4,2,6,2048]{3,1,2,0:T(2,128)S(1)}, u32[]{:S(2)}, u32[]{:S(2)}) %all-to-all-start) | async-done | bytes 393248 | tf_op jit(solution)/shard_map/all_to_all | solution.py:88
  221.4 2.0 fusion.62
  223.6 7.1 %broadcast_multiply_fusion = (f32[5,8,64,256]{3,2,1,0:T(8,128)S(1)}, f32[5,8,64,256]{3,2,1,0:T(8,128)S(1)}) fusion(f32[8,64,256]{2,1,0:T(8,128)} %copy-done.6, f32[5,8,64,256]{3,2,1,0:T(8,128)S(1)} %bitcast.79, f32[1,8,64,256]{3,2,1,0:T(8,128)S(1)} %get-tuple-element.254, f32[3,8,64,256]{3,2,1,0:T(8,128)S(1)} %broadcast_in_dim.13, f32[5]{0:T(128)S(1)} %pad.16.clone, ...), kind=kLoop, calls=%fused_computation.65 | loop fusion | flops 17694720 | bytes 14410004 | tf_op jit(solution)/shard_map/mul | solution.py:56
  231.8 2.3 fusion.61
  234.1 1.5 collective-permute-start.5
  237.5 4.5 %collective-permute-start.8 = (f32[5,8,1,256]{3,2,1,0:T(1,128)S(1)}, f32[5,8,1,256]{3,2,1,0:T(1,128)S(1)}, u32[]{:S(2)}, u32[]{:S(2)}) collective-permute-start(f32[5,8,1,256]{3,2,1,0:T(1,128)S(1)} %get-tuple-element.243), channel_id=1, source_target_pairs={{0,1},{1,2},{2,3},{4,5},{5,6},{6,7},{8,9},{9,10},{10,11},{12,13},{... | collective-permute-start | bytes 122888 | tf_op jit(solution)/shard_map/ppermute | solution.py:20
  242.1 2.0 fusion.58
  244.1 1.8 broadcast_in_dim_reshape.3
  245.9 5.2 %collective-permute-done.6 = f32[5,1,64,256]{3,2,1,0:T(8,128)} collective-permute-done((f32[5,1,64,256]{3,2,1,0:T(8,128)}, f32[5,1,64,256]{3,2,1,0:T(8,128)}, u32[]{:S(2)}, u32[]{:S(2)}) %collective-permute-start.6) | collective-permute-done | bytes 327712 | tf_op jit(solution)/shard_map/ppermute | solution.py:20
  251.1 14.8 %fusion.9 = f32[1,5,8,64,256]{4,3,2,1,0:T(8,128)} fusion(f32[5,8,64,256]{3,2,1,0:T(8,128)} %copy-done.3, f32[5,8,64,1]{3,2,1,0:T(8,128)} %get-tuple-element.245, f32[5,8,64,1]{3,2,1,0:T(8,128)} %get-tuple-element.244, f32[5,8,1,256]{3,2,1,0:T(1,128)S(1)} %collective-permute-done.8, f32[5,8,1,256]{3,2,1,0:T(1,128)S(1)} %collective-permute-done.7, ...), kind=kLoop, calls=%fused_computation.25 | loop fusion | flops 18350080 | bytes 13885716 | tf_op jit(solution)/shard_map/broadcast_in_dim | solution.py:166
  (241 shorter events, 54.5 us)
Async XLA Ops:
  7.2 162.7 %copy-start = (s32[1,32]{1,0:T(1,128)S(1)}, s32[1,32]{1,0:T(1,128)}, u32[]{:S(2)}) copy-start(s32[1,32]{1,0:T(1,128)} %param.15) | copy-start | bytes 388
  7.2 189.6 %all-gather.3.cloned.1.call-start = ((), (), s32[]{:S(2)}) async-start(), calls=%async_computation.1 | async-start | bytes 1966080 | tf_op jit(solution)/shard_map/all_gather | solution.py:130
  84.8 0.7 copy-start.10
  155.1 14.3 %copy-start.9 = (s32[1,32]{1,0:T(1,128)S(1)}, s32[1,32]{1,0:T(1,128)}, u32[]{:S(2)}) copy-start(s32[1,32]{1,0:T(1,128)} %param.14) | copy-start | bytes 388
  157.6 65.7 %collective-permute-start.3 = (f32[5,8,1,256]{3,2,1,0:T(1,128)}, f32[5,8,1,256]{3,2,1,0:T(1,128)S(1)}, u32[]{:S(2)}, u32[]{:S(2)}) collective-permute-start(f32[5,8,1,256]{3,2,1,0:T(1,128)} %get-tuple-element.250), channel_id=1, source_target_pairs={{1,0},{2,1},{3,2},{5,4},{6,5},{7,6},{9,8},{10,9},{11,10},{13,12},{... | collective-permute-start | bytes 122888 | tf_op jit(solution)/shard_map/ppermute | solution.py:23
  158.9 64.5 %collective-permute-start.4 = (f32[5,8,1,256]{3,2,1,0:T(1,128)S(1)}, f32[5,8,1,256]{3,2,1,0:T(1,128)S(1)}, u32[]{:S(2)}, u32[]{:S(2)}) collective-permute-start(f32[5,8,1,256]{3,2,1,0:T(1,128)S(1)} %get-tuple-element.251), channel_id=1, source_target_pairs={{0,1},{1,2},{2,3},{4,5},{5,6},{6,7},{8,9},{9,10},{10,11},{12,13},{... | collective-permute-start | bytes 122888 | tf_op jit(solution)/shard_map/ppermute | solution.py:20
  166.5 56.9 %collective-permute-start.1 = (f32[5,1,64,256]{3,2,1,0:T(8,128)}, f32[5,1,64,256]{3,2,1,0:T(8,128)}, u32[]{:S(2)}, u32[]{:S(2)}) collective-permute-start(f32[5,1,64,256]{3,2,1,0:T(8,128)} %get-tuple-element.248), channel_id=1, source_target_pairs={{4,0},{8,4},{12,8},{0,12},{5,1},{9,5},{13,9},{1,13},{6,2},{10,6},{... | collective-permute-start | bytes 983048 | tf_op jit(solution)/shard_map/ppermute | solution.py:23
  169.4 54.0 %collective-permute-start.2 = (f32[5,1,64,256]{3,2,1,0:T(8,128)}, f32[5,1,64,256]{3,2,1,0:T(8,128)}, u32[]{:S(2)}, u32[]{:S(2)}) collective-permute-start(f32[5,1,64,256]{3,2,1,0:T(8,128)} %get-tuple-element.249), channel_id=1, source_target_pairs={{0,4},{4,8},{8,12},{12,0},{1,5},{5,9},{9,13},{13,1},{2,6},{6,10},{... | collective-permute-start | bytes 983048 | tf_op jit(solution)/shard_map/ppermute | solution.py:20
  198.4 1.8 collective-permute-start
  201.5 16.1 %all-to-all-start = ((f32[4,2,6,2048]{3,1,2,0:T(2,128)}), f32[4,2,6,2048]{3,1,2,0:T(2,128)S(1)}, u32[]{:S(2)}, u32[]{:S(2)}) async-start(f32[4,2,6,2048]{3,1,2,0:T(2,128)} %fusion.48), calls=%async_computation | async-start | bytes 786432 | tf_op jit(solution)/shard_map/all_to_all | solution.py:88
  218.2 0.7 copy-start.7
  219.1 1.9 copy-start.1
  219.8 1.6 copy-start.6
  221.4 2.2 copy-start.8
  223.6 7.2 %copy-start.5 = (f32[3,8,64,256]{3,2,1,0:T(8,128)}, f32[3,8,64,256]{3,2,1,0:T(8,128)S(1)}, u32[]{:S(2)}) copy-start(f32[3,8,64,256]{3,2,1,0:T(8,128)S(1)} %broadcast_in_dim.13) | copy-start | bytes 4718596
  230.8 5.4 %copy-start.3 = (f32[5,8,64,256]{3,2,1,0:T(8,128)}, f32[5,8,64,256]{3,2,1,0:T(8,128)S(1)}, u32[]{:S(2)}) copy-start(f32[5,8,64,256]{3,2,1,0:T(8,128)S(1)} %get-tuple-element.235) | copy-start | bytes 7864324
  230.8 11.3 %copy-start.4 = (f32[5,8,64,256]{3,2,1,0:T(8,128)}, f32[5,8,64,256]{3,2,1,0:T(8,128)S(1)}, u32[]{:S(2)}) copy-start(f32[5,8,64,256]{3,2,1,0:T(8,128)S(1)} %get-tuple-element.234) | copy-start | bytes 7864324
  234.1 11.8 %collective-permute-start.5 = (f32[5,1,64,256]{3,2,1,0:T(8,128)}, f32[5,1,64,256]{3,2,1,0:T(8,128)}, u32[]{:S(2)}, u32[]{:S(2)}) collective-permute-start(f32[5,1,64,256]{3,2,1,0:T(8,128)} %get-tuple-element.240), channel_id=1, source_target_pairs={{4,0},{8,4},{12,8},{0,12},{5,1},{9,5},{13,9},{1,13},{6,2},{10,6},{... | collective-permute-start | bytes 983048 | tf_op jit(solution)/shard_map/ppermute | solution.py:23
  235.6 15.5 %collective-permute-start.6 = (f32[5,1,64,256]{3,2,1,0:T(8,128)}, f32[5,1,64,256]{3,2,1,0:T(8,128)}, u32[]{:S(2)}, u32[]{:S(2)}) collective-permute-start(f32[5,1,64,256]{3,2,1,0:T(8,128)} %get-tuple-element.241), channel_id=1, source_target_pairs={{0,4},{4,8},{8,12},{12,0},{1,5},{5,9},{9,13},{13,1},{2,6},{6,10},{... | collective-permute-start | bytes 983048 | tf_op jit(solution)/shard_map/ppermute | solution.py:20
  236.2 9.7 %collective-permute-start.7 = (f32[5,8,1,256]{3,2,1,0:T(1,128)S(1)}, f32[5,8,1,256]{3,2,1,0:T(1,128)S(1)}, u32[]{:S(2)}, u32[]{:S(2)}) collective-permute-start(f32[5,8,1,256]{3,2,1,0:T(1,128)S(1)} %get-tuple-element.242), channel_id=1, source_target_pairs={{1,0},{2,1},{3,2},{5,4},{6,5},{7,6},{9,8},{10,9},{11,10},{13,12},{... | collective-permute-start | bytes 122888 | tf_op jit(solution)/shard_map/ppermute | solution.py:23
  237.5 8.4 %collective-permute-start.8 = (f32[5,8,1,256]{3,2,1,0:T(1,128)S(1)}, f32[5,8,1,256]{3,2,1,0:T(1,128)S(1)}, u32[]{:S(2)}, u32[]{:S(2)}) collective-permute-start(f32[5,8,1,256]{3,2,1,0:T(1,128)S(1)} %get-tuple-element.243), channel_id=1, source_target_pairs={{0,1},{1,2},{2,3},{4,5},{5,6},{6,7},{8,9},{9,10},{10,11},{12,13},{... | collective-permute-start | bytes 122888 | tf_op jit(solution)/shard_map/ppermute | solution.py:20
  242.1 9.0 %copy-start.2 = (f32[1,5,8,64,256]{4,3,2,1,0:T(8,128)S(1)}, f32[1,5,8,64,256]{4,3,2,1,0:T(8,128)}, u32[]{:S(2)}) copy-start(f32[1,5,8,64,256]{4,3,2,1,0:T(8,128)} %param.12) | copy-start | bytes 7864324
Sparse Core Ops, SparseCore 0:
  156.0 40.7 all-gather.2
